TPU v7x, 256 devices: a whole 4x4x8 slice. The times are simulated.
256 devices in a mesh: edp: 8 (over z_lo, x), ep: 32 (over y, z_hi, core).
Axes of the slice: x: 4, y: 4, z: 8 (z_hi: 4, z_lo: 2; z = z_hi * 2 + z_lo), core: 2. Of those that a mesh axis runs over, the one named last changes fastest.
Arguments:
- attn_input: bfloat16 [32768, 3584], P(('edp', 'ep')), may hold values from -24 to 24
- kv_gain: float32 [3584], replicated, may hold values from 0.25 to 1.75
- latent_cot: bfloat16 [32768, 512], P(('edp', 'ep')), may hold values from -0.03125 to 0.03125
- attn_resid: float32 [3584, 512], P(('edp', 'ep')), may hold values from -4 to 4
- moe_input: bfloat16 [32768, 3584], P(('edp', 'ep')), may hold values from -24 to 24
- moe_cot: bfloat16 [32768, 3584], P(('edp', 'ep')), may hold values from -0.0625 to 0.0625
- expert_ids: int32 [32768, 2], P(('edp', 'ep')), may hold values from 0 to 7, all different within a row; in each aligned block of 128 rows (0 to 127, 128 to 255, ...) at most 40 rows name the same one
- gate_probs: float32 [32768, 2], P(('edp', 'ep')), may hold values from 0.2 to 1
- w_gate: bfloat16 [3584, 8192], P(None, 'ep'), may hold values from -0.09375 to 0.09375
- w_up: bfloat16 [3584, 8192], P(None, 'ep'), may hold values from -0.09375 to 0.09375
- w_down: bfloat16 [8192, 3584], P('ep'), may hold values from -0.1875 to 0.1875
- gate_resid: float32 [3584, 8192], P('edp', 'ep'), may hold values from -4 to 4
- up_resid: float32 [3584, 8192], P('edp', 'ep'), may hold values from -4 to 4
- down_resid: float32 [8192, 3584], P('ep', 'edp'), may hold values from -4 to 4
Outputs:
- kv_grad: bfloat16 [3584, 512], P(('edp', 'ep'))
- gate_grad: bfloat16 [3584, 8192], P('edp', 'ep')
- up_grad: bfloat16 [3584, 8192], P('edp', 'ep')
- down_grad: bfloat16 [8192, 3584], P('ep', 'edp')
Inputs may be any that keep to these rules, and one draw needn't show every extreme that they name: `expert_ids`: each row names 2 different experts. Among the rows of one device no expert is named more than 40 times, and in some devices' rows one is named exactly 40 times.
All inputs are finite; a program needn't handle non-finite values.
Results may differ from a plain program's by a relative error of at most 0.019.
Values may be sent and summed in bfloat16 or wider, within the bound.
A program may use at most 128 MiB of HBM per device.

v0:
```python
import jax
import jax.numpy as jnp
from jax import lax
from jax.sharding import Mesh
from jax.sharding import PartitionSpec as P

TOP = 2
SPLIT = 4
EDP_EP = ("edp_0", "edp_1", "ep_0", "ep_1", "ep_2")
EP = ("ep_0", "ep_1", "ep_2")
EDP = ("edp_0", "edp_1")


epsilon = 1e-06


def split_up(shard, dim, count):
    before, after = (shard.shape[:dim], shard.shape[dim + 1 :])
    return jnp.moveaxis(shard.reshape(*before, count, -1, *after), dim, 0)


def summed_rows(shard, chips, core, dim):
    sizes = (lax.axis_size(chips), lax.axis_size(core))
    parts = split_up(shard, dim, sizes[0] * sizes[1])
    inside = parts.shape[1:]
    parts = parts.reshape(*sizes, *inside).swapaxes(0, 1).reshape(-1, *inside)
    parts = lax.psum_scatter(parts, core, scatter_dimension=0, tiled=True)
    return lax.psum_scatter(parts, chips, scatter_dimension=0, tiled=True)[0]


def contract_rows(left, right):
    return lax.dot_general(
        left, right, (((0,), (0,)), ((), ())), preferred_element_type=jnp.float32
    )


def latent_gradient(attn_input, kv_gain, latent_cot, attn_resid):
    values = attn_input.astype(jnp.float32)
    inv_rms = lax.rsqrt(jnp.mean(values * values, axis=1, keepdims=True) + epsilon)
    normed = (values * inv_rms * kv_gain[None, :]).astype(jnp.bfloat16)
    summed = summed_rows(
        contract_rows(normed, latent_cot), ("edp_0", "edp_1", "ep_0", "ep_1"), "ep_2", 0
    )
    return (summed + attn_resid).astype(jnp.bfloat16)


def slot_tables(expert_ids, gate_probs, experts, capacity):
    labels = jnp.arange(experts, dtype=jnp.int32)
    one_hot = (expert_ids[:, :, None] == labels[None, None, :]).astype(jnp.int32)
    chosen = jnp.sum(one_hot, axis=1)
    weight = jnp.sum(one_hot.astype(jnp.float32) * gate_probs[:, :, None], axis=1)
    position = jnp.cumsum(chosen, axis=0) - chosen
    slot_ids = jnp.arange(capacity, dtype=jnp.int32)
    dispatch = (chosen[None, :, :] > 0) & (position[None, :, :] == slot_ids[:, None, None])
    return (jnp.transpose(dispatch, (2, 0, 1)), weight)


def forward_part(rows_in, w_gate, w_up):
    gate_proj = jnp.dot(rows_in, w_gate, preferred_element_type=jnp.float32)
    up_proj = jnp.dot(rows_in, w_up, preferred_element_type=jnp.float32)
    return (gate_proj, up_proj)


def backward_part(rows_in, rows_cot, gate_proj, up_proj, w_down):
    sigmoid_gate = jax.nn.sigmoid(gate_proj)
    active = (gate_proj * sigmoid_gate * up_proj).astype(jnp.bfloat16)
    back_grad = lax.dot_general(
        rows_cot, w_down, (((1,), (1,)), ((), ())), preferred_element_type=jnp.float32
    )
    up_rows = (back_grad * gate_proj * sigmoid_gate).astype(jnp.bfloat16)
    gate_rows = (
        back_grad * up_proj * sigmoid_gate * (1.0 + gate_proj * (1.0 - sigmoid_gate))
    ).astype(jnp.bfloat16)
    return (
        contract_rows(rows_in, gate_rows),
        contract_rows(rows_in, up_rows),
        contract_rows(active, rows_cot),
    )


def body(
    attn_input,
    kv_gain,
    latent_cot,
    attn_resid,
    moe_input,
    moe_cot,
    expert_ids,
    gate_probs,
    w_gate,
    w_up,
    w_down,
    gate_resid,
    up_resid,
    down_resid,
):
    experts = lax.axis_size(EP) // SPLIT
    capacity = 5 * moe_input.shape[0] * TOP // (4 * experts)
    model_width = moe_input.shape[1]
    dispatch, weight = slot_tables(expert_ids, gate_probs, experts, capacity)
    dispatch_half = dispatch.astype(jnp.bfloat16)
    sent_in = jnp.einsum(
        "ect,td->ecd", dispatch_half, moe_input, preferred_element_type=jnp.float32
    ).astype(jnp.bfloat16)
    sent_cot = jnp.einsum("ect,td->ecd", dispatch_half, moe_cot, preferred_element_type=jnp.float32)
    slot_weight = jnp.einsum("ect,te->ec", dispatch.astype(jnp.float32), weight)
    sent_cot = (sent_cot * slot_weight[:, :, None]).astype(jnp.bfloat16)
    sent_in = jnp.repeat(sent_in, SPLIT, axis=0)
    sent_cot = jnp.repeat(sent_cot, SPLIT, axis=0)
    got_in = lax.all_to_all(sent_in, EP, split_axis=0, concat_axis=0, tiled=True)
    rows_in = got_in.reshape(-1, model_width)
    gate_proj, up_proj = forward_part(rows_in, w_gate, w_up)
    got_cot = lax.all_to_all(sent_cot, EP, split_axis=0, concat_axis=0, tiled=True)
    rows_cot = got_cot.reshape(-1, model_width)
    term_gate, term_up, term_down = backward_part(rows_in, rows_cot, gate_proj, up_proj, w_down)
    sum_gate, sum_up = (
        lax.psum_scatter(
            term_gate.astype(jnp.bfloat16), EDP, scatter_dimension=0, tiled=True
        ).astype(jnp.float32),
        lax.psum_scatter(term_up.astype(jnp.bfloat16), EDP, scatter_dimension=0, tiled=True).astype(
            jnp.float32
        ),
    )
    sum_down = lax.psum_scatter(
        term_down.astype(jnp.bfloat16), EDP, scatter_dimension=1, tiled=True
    ).astype(jnp.float32)
    gate_grad = (sum_gate + gate_resid).astype(jnp.bfloat16)
    up_grad = (sum_up + up_resid).astype(jnp.bfloat16)
    down_grad = (sum_down + down_resid).astype(jnp.bfloat16)
    kv_grad = latent_gradient(attn_input, kv_gain, latent_cot, attn_resid)
    return (kv_grad, gate_grad, up_grad, down_grad)


def solution(mesh):
    torus = Mesh(mesh.devices.reshape(2, 4, 4, 4, 2), ("edp_0", "edp_1", "ep_0", "ep_1", "ep_2"))
    return jax.shard_map(
        body,
        mesh=torus,
        in_specs=(
            P(EDP_EP, None),
            P(),
            P(EDP_EP, None),
            P(EDP_EP, None),
            P(EDP_EP, None),
            P(EDP_EP, None),
            P(EDP_EP, None),
            P(EDP_EP, None),
            P(None, EP),
            P(None, EP),
            P(EP, None),
            P(EDP, EP),
            P(EDP, EP),
            P(EP, EDP),
        ),
        out_specs=(P(EDP_EP, None), P(EDP, EP), P(EDP, EP), P(EP, EDP)),
        check_vma=False,
    )
```

profile of v0, /device:TPU:1, one launch (start us, length us, event | category | flops | bytes accessed | tf_op | source)
XLA Modules:
  0.0 662.2 jit_solution(10577115472157211680)
XLA Ops:
  8.0 0.0 copy-start
  8.0 0.8 convert_reduce_fusion
  8.8 0.1 copy.38
  8.9 0.2 reduce_window_sum.11
  9.2 1.9 convolution_convert_fusion
  11.1 4.2 broadcast_in_dim.4
  15.4 12.9 %all-to-all-start = ((bf16[32,40,3584]{2,1,0:T(8,128)(2,1)}), bf16[32,40,3584]{2,1,0:T(8,128)(2,1)}, u32[]{:S(2)}, u32[]{:S(2)}) async-start(bf16[32,40,3584]{2,1,0:T(8,128)(2,1)} %bitcast.38), calls=%async_computation.1 | async-start | bytes 18350080 | tf_op jit(solution)/shard_map/all_to_all | solution.py:110
  28.3 0.2 fusion.14
  28.5 2.2 fusion
  30.7 201.1 %all-to-all-done = bf16[32,40,3584]{2,1,0:T(8,128)(2,1)} async-done(((bf16[32,40,3584]{2,1,0:T(8,128)(2,1)}), bf16[32,40,3584]{2,1,0:T(8,128)(2,1)}, u32[]{:S(2)}, u32[]{:S(2)}) %all-to-all-start) | async-done | bytes 9175072 | tf_op jit(solution)/shard_map/all_to_all | solution.py:110
  231.8 6.0 broadcast_in_dim.5
  237.7 6.4 all-to-all-start.1
  244.1 0.0 reduce-scatter.6.cloned.1.call-start
  244.2 0.3 fusion.1
  244.5 4.2 fusion.4
  248.7 9.0 %reshape_reshape.3 = f32[128,2,14,512]{3,2,1,0:T(8,128)} reshape(f32[3584,512]{1,0:T(8,128)} %fusion.4) | data formatting | bytes 14680064 | tf_op jit(solution)/shard_map/reshape;reshape | solution.py:26
  257.7 10.6 %copy.37 = f32[2,128,14,512]{3,1,0,2:T(8,128)} copy(f32[2,128,14,512]{3,2,0,1:T(8,128)} %bitcast.39) | data formatting | bytes 14680064 | tf_op jit(solution)/shard_map/transpose | solution.py:26
  268.4 0.0 reduce-scatter.6.cloned.1.call-update
  268.4 0.0 all-reduce.3.cloned.1.call-start
  268.4 22.9 %reduce-scatter.6.cloned.1.call-done = f32[128,14,512]{2,0,1:T(8,128)} async-done(((f32[256,14,512]{2,0,1:T(8,128)}), f32[128,14,512]{2,0,1:T(8,128)}) %reduce-scatter.6.cloned.1.call-update) | async-done | bytes 3670032 | tf_op jit(solution)/shard_map/reduce_scatter | solution.py:27
  291.3 0.0 all-reduce.3.cloned.1.call-update
  291.4 0.2 reduce-scatter.8.cloned.1.call-start
  291.6 0.0 copy-start.12
  291.6 6.3 fusion.32
  297.9 0.0 copy-start.13
  297.9 7.3 %fusion.31 = f32[1280,256]{1,0:T(8,128)} fusion(bf16[1280,3584]{1,0:T(8,128)(2,1)} %bitcast.6, bf16[3584,256]{1,0:T(8,128)(2,1)S(1)} %copy-done.12), kind=kOutput, calls=%fused_computation.50 | convolution fusion | flops 2348810240 | bytes 12320768 | tf_op jit(solution)/shard_map/dot_general | solution.py:60
  305.3 159.5 %all-to-all-done.1 = bf16[32,40,3584]{2,1,0:T(8,128)(2,1)} async-done(((bf16[32,40,3584]{2,1,0:T(8,128)(2,1)}), bf16[32,40,3584]{2,1,0:T(8,128)(2,1)}, u32[]{:S(2)}, u32[]{:S(2)}) %all-to-all-start.1) | async-done | bytes 9175072 | tf_op jit(solution)/shard_map/all_to_all | solution.py:113
  464.8 6.4 fusion.30
  471.2 1.1 copy-done.17
  472.3 7.7 %convolution_convert_fusion.3 = bf16[3584,256]{1,0:T(8,128)(2,1)} fusion(bf16[1280,3584]{1,0:T(8,128)(2,1)} %bitcast.6, f32[1280,256]{1,0:T(8,128)S(1)} %fusion.32, f32[1280,256]{1,0:T(8,128)S(1)} %fusion.30, f32[1280,256]{1,0:T(8,128)S(1)} %copy-done.15), kind=kOutput, calls=%fused_computation.5 | convolution fusion | flops 2353004544 | bytes 14942208 | tf_op jit(solution)/shard_map/dot_general | solution.py:32
  480.0 0.0 reduce-scatter.8.cloned.1.call-update
  480.0 0.3 reduce-scatter.12.cloned.1.call-start
  480.3 1.0 copy-done.16
  481.3 8.7 %convolution_convert_fusion.1 = bf16[256,3584]{0,1:T(8,128)(2,1)} fusion(bf16[1280,3584]{1,0:T(8,128)(2,1)} %bitcast.13, f32[1280,256]{1,0:T(8,128)S(1)} %copy-done.16, f32[1280,256]{1,0:T(8,128)S(1)} %fusion.32), kind=kOutput, calls=%fused_computation.3 | convolution fusion | flops 2351693824 | bytes 13631488 | tf_op jit(solution)/shard_map/dot_general | solution.py:32
  490.0 0.0 reduce-scatter.12.cloned.1.call-update
  490.0 0.0 reduce-scatter.10.cloned.1.call-start
  490.1 1.2 copy-done.18
  491.3 7.6 %convolution_convert_fusion.2 = bf16[3584,256]{1,0:T(8,128)(2,1)} fusion(bf16[1280,3584]{1,0:T(8,128)(2,1)} %bitcast.6, f32[1280,256]{1,0:T(8,128)S(1)} %copy-done.18, f32[1280,256]{1,0:T(8,128)S(1)} %fusion.32), kind=kOutput, calls=%fused_computation.4 | convolution fusion | flops 2351693824 | bytes 13631488 | tf_op jit(solution)/shard_map/dot_general | solution.py:32
  499.0 0.0 reduce-scatter.10.cloned.1.call-update
  499.0 0.0 copy-start.1
  499.0 0.6 copy-done.14
  499.6 0.6 dynamic-slice
  500.2 147.1 %all-reduce.3.cloned.1.call-done = f32[128,14,512]{2,0,1:T(8,128)} async-done(((f32[128,14,512]{2,0,1:T(8,128)}), f32[128,14,512]{2,0,1:T(8,128)}) %all-reduce.3.cloned.1.call-update) | async-done | bytes 3670032
  647.3 1.6 constant_dynamic-slice_fusion
  648.9 0.6 fusion.24
  649.5 1.7 add_convert_fusion.2
  651.2 1.7 add_convert_fusion
  652.9 1.7 add_convert_fusion.1
  (38 shorter events, 0.1 us)
Async XLA Ops:
  8.0 283.6 %copy-start = (bf16[3584,256]{1,0:T(8,128)(2,1)S(1)}, bf16[3584,256]{1,0:T(8,128)(2,1)}, u32[]{:S(2)}) copy-start(bf16[3584,256]{1,0:T(8,128)(2,1)} %param.22) | copy-start | bytes 5505028
  15.4 13.0 %copy-start.10 = (s32[128,2]{0,1:T(2,128)S(1)}, s32[128,2]{0,1:T(2,128)}, u32[]{:S(2)}) copy-start(s32[128,2]{0,1:T(2,128)} %param.20) | copy-start | bytes 3076
  15.4 13.0 %copy-start.11 = (f32[128,2]{0,1:T(2,128)S(1)}, f32[128,2]{0,1:T(2,128)}, u32[]{:S(2)}) copy-start(f32[128,2]{0,1:T(2,128)} %param.21) | copy-start | bytes 3076
  15.4 13.1 %copy-start.3 = (bf16[128,3584]{1,0:T(8,128)(2,1)S(1)}, bf16[128,3584]{1,0:T(8,128)(2,1)}, u32[]{:S(2)}) copy-start(bf16[128,3584]{1,0:T(8,128)(2,1)} %param.19) | copy-start | bytes 2752516
  15.4 216.4 %all-to-all-start = ((bf16[32,40,3584]{2,1,0:T(8,128)(2,1)}), bf16[32,40,3584]{2,1,0:T(8,128)(2,1)}, u32[]{:S(2)}, u32[]{:S(2)}) async-start(bf16[32,40,3584]{2,1,0:T(8,128)(2,1)} %bitcast.38), calls=%async_computation.1 | async-start | bytes 18350080 | tf_op jit(solution)/shard_map/all_to_all | solution.py:110
  237.7 6.5 copy-start.2
  237.7 6.8 %copy-start.7 = (bf16[128,512]{1,0:T(8,128)(2,1)S(1)}, bf16[128,512]{1,0:T(8,128)(2,1)}, u32[]{:S(2)}) copy-start(bf16[128,512]{1,0:T(8,128)(2,1)} %param.16) | copy-start | bytes 393220
  237.7 6.8 %copy-start.8 = (f32[3584]{0:T(1024)S(1)}, f32[3584]{0:T(1024)}, u32[]{:S(2)}) copy-start(f32[3584]{0:T(1024)} %param.15) | copy-start | bytes 43012
  237.7 227.1 %all-to-all-start.1 = ((bf16[32,40,3584]{2,1,0:T(8,128)(2,1)}), bf16[32,40,3584]{2,1,0:T(8,128)(2,1)}, u32[]{:S(2)}, u32[]{:S(2)}) async-start(bf16[32,40,3584]{2,1,0:T(8,128)(2,1)} %bitcast.37), calls=%async_computation.2 | async-start | bytes 18350080 | tf_op jit(solution)/shard_map/all_to_all | solution.py:113
  244.1 47.2 %reduce-scatter.6.cloned.1.call-start = ((), (), s32[]{:S(2)}) async-start(), calls=%async_computation.6 | async-start | bytes 11010048 | tf_op jit(solution)/shard_map/reduce_scatter | solution.py:27
  268.4 378.9 %all-reduce.3.cloned.1.call-start = ((), (), s32[]{:S(2)}) async-start(), calls=%async_computation.10 | async-start | bytes 7340032
  291.4 358.2 %reduce-scatter.8.cloned.1.call-start = ((), (), s32[]{:S(2)}) async-start(), calls=%async_computation.7 | async-start | bytes 2064384 | tf_op jit(solution)/shard_map/reduce_scatter | solution.py:117
  291.6 6.3 copy-start.12
  297.9 166.9 %copy-start.13 = (bf16[256,3584]{1,0:T(8,128)(2,1)S(1)}, bf16[256,3584]{1,0:T(8,128)(2,1)}, u32[]{:S(2)}) copy-start(bf16[256,3584]{1,0:T(8,128)(2,1)} %param.24) | copy-start | bytes 5505028
  464.8 7.5 %copy-start.15 = (f32[1280,256]{1,0:T(8,128)S(1)}, f32[1280,256]{1,0:T(8,128)}, u32[]{:S(2)}) copy-start(f32[1280,256]{1,0:T(8,128)} %fusion.31) | copy-start | bytes 3932164
  471.2 1.1 copy-start.17
  480.0 1.3 copy-start.16
  480.0 171.2 %reduce-scatter.12.cloned.1.call-start = ((), (), s32[]{:S(2)}) async-start(), calls=%async_computation.9 | async-start | bytes 2064384 | tf_op jit(solution)/shard_map/reduce_scatter | solution.py:124
  490.0 1.3 copy-start.18
  490.0 162.9 %reduce-scatter.10.cloned.1.call-start = ((), (), s32[]{:S(2)}) async-start(), calls=%async_computation.8 | async-start | bytes 2064384 | tf_op jit(solution)/shard_map/reduce_scatter | solution.py:120
  498.9 0.7 copy-start.14
  498.9 150.0 %copy-start.9 = (f32[14,512]{1,0:T(8,128)S(1)}, f32[14,512]{1,0:T(8,128)}, u32[]{:S(2)}) copy-start(f32[14,512]{1,0:T(8,128)} %param.17) | copy-start | bytes 86020
  498.9 150.6 %copy-start.4 = (f32[448,256]{1,0:T(8,128)S(1)}, f32[448,256]{1,0:T(8,128)}, u32[]{:S(2)}) copy-start(f32[448,256]{1,0:T(8,128)} %param.25) | copy-start | bytes 1376260
  498.9 152.3 %copy-start.5 = (f32[256,448]{0,1:T(8,128)S(1)}, f32[256,448]{0,1:T(8,128)}, u32[]{:S(2)}) copy-start(f32[256,448]{0,1:T(8,128)} %param.27) | copy-start | bytes 1376260
  498.9 154.0 %copy-start.6 = (f32[448,256]{1,0:T(8,128)S(1)}, f32[448,256]{1,0:T(8,128)}, u32[]{:S(2)}) copy-start(f32[448,256]{1,0:T(8,128)} %param.26) | copy-start | bytes 1376260
  499.0 155.6 %copy-start.1 = (bf16[3584,256]{1,0:T(8,128)(2,1)S(1)}, bf16[3584,256]{1,0:T(8,128)(2,1)}, u32[]{:S(2)}) copy-start(bf16[3584,256]{1,0:T(8,128)(2,1)} %param.22) | copy-start | bytes 5505028
Sparse Core Ops, SparseCore 0:
  268.5 22.7 reduce-scatter.5
  297.8 349.4 all-reduce.2
Sparse Core Ops, SparseCore 1:
  480.1 36.4 reduce-scatter.7
  519.2 43.1 reduce-scatter.11
  565.0 43.8 reduce-scatter.9
where the time goes:
time: 666 us; the launch traced here: 662 us
  waiting for transfers between devices  531 us (80%)
  matrix products  52.5 us (8%)
  local copies, waits for them, and re-layouts  36.2 us (5%)
  starting transfers between devices  20 us (3%)
  between operations  15.9 us (2%)
  other arithmetic  6.93 us (1%)
    all_to_all x1, waiting for transfers between devices, body(): lax.all_to_all(sent_in, EP, split_axis=0, concat_axis=0, tiled=True)  201 us
    all_to_all x1, waiting for transfers between devices, body(): lax.all_to_all(sent_cot, EP, split_axis=0, concat_axis=0, tiled=True)  160 us
    unnamed x6, waiting for transfers between devices  147 us
    dot_general x4, matrix products, contract_rows(): lax.dot_general(left, right, (((0,), (0,)), ((), ())), preferred_element_...  28.2 us
    reduce_scatter x1, waiting for transfers between devices, summed_rows(): parts = lax.psum_scatter(parts, core, scatter_dimension=0, tiled=True)  22.9 us
  transfers between devices with their start and end apart: 7, of which 4 were waited for; matrix products, arithmetic and copies ran while one was open for 12% of the time, Pallas kernels for 0%

commit v1 on v0

v1 whole, which is shorter than its diff:
```python
import jax
import jax.numpy as jnp
from jax import lax
from jax.experimental import pallas as pl
from jax.experimental.pallas import tpu as pltpu
from jax.sharding import Mesh
from jax.sharding import PartitionSpec as P

MESH = pl.DeviceIdType.MESH
EDP_EP = ("edp_0", "edp_1", "ep_0", "ep_1", "ep_2")
EP = ("ep_0", "ep_1", "ep_2")
EDP = ("edp_0", "edp_1")
F32, BF16 = jnp.float32, jnp.bfloat16

epsilon = 1e-06

D, TOK, FQ, CAP, KVL = 3584, 128, 256, 40, 512
EXPERTS = 8
BLOCK = 2 * CAP
CHUNK = 4 * BLOCK
ROWS = 4 * CHUNK
PIECES = 2
WIDE = D // PIECES
PAIR = 896
SLICE = 2688
COPIES = 96


def kernel(
    ids_ref,
    probs_ref,
    gain_ref,
    input_hbm,
    cot_hbm,
    attn_hbm,
    latent_hbm,
    w_gate_hbm,
    w_up_hbm,
    w_down_hbm,
    kv_out,
    terms_out,
    own,
    tokens,
    meta,
    ready,
    passing,
    rows,
    w_gate_up,
    w_down,
    latent,
    hidden_t,
    work,
    parts,
    first_sums,
    second_sums,
    last_sum,
    kv_core,
    kv_x,
    kv_x_sum,
    kv_y,
    kv_y_sum,
    kv_z,
    send_sems,
    recv_sems,
    load_sems,
):
    zl, x, y = lax.axis_index("edp_0"), lax.axis_index("edp_1"), lax.axis_index("ep_0")
    zh, c = lax.axis_index("ep_1"), lax.axis_index("ep_2")
    z = zh * 2 + zl
    other = 1 - c

    def at_z(target):
        return (lax.rem(target, 2), x, y, target // 2, c)

    def at_y(target):
        return (zl, x, target, zh, c)

    def at_x(target):
        return (zl, target, y, zh, c)

    other_core = (zl, x, y, zh, other)
    other_zl = (1 - zl, x, y, zh, c)

    used = [0]

    def remote(src, dst, device, index=None):
        if index is None:
            index = used[0]
            used[0] += 1
        return pltpu.make_async_remote_copy(
            src_ref=src,
            dst_ref=dst,
            send_sem=send_sems.at[index],
            recv_sem=recv_sems.at[index],
            device_id=device,
            device_id_type=MESH,
        )

    loads = [0]

    def local(src, dst):
        copy = pltpu.make_async_copy(src, dst, load_sems.at[loads[0]])
        loads[0] += 1
        return copy

    load_own = [local(input_hbm, own.at[0]), local(cot_hbm, own.at[1])]
    load_later = [
        local(w_gate_hbm, w_gate_up.at[:, pl.ds(0, FQ)]),
        local(w_up_hbm, w_gate_up.at[:, pl.ds(FQ, FQ)]),
        local(w_down_hbm, w_down),
    ]
    load_latent = local(latent_hbm, latent)
    for copy in load_own + load_later + [load_latent]:
        copy.start()

    barrier = pltpu.get_barrier_semaphore()
    partners = [other_core]
    partners += [at_z(lax.rem(z + step, 8)) for step in range(1, 8)]
    partners += [at_y(lax.rem(y + step, 4)) for step in range(1, 4)]
    partners += [at_x(lax.rem(x + step, 4)) for step in range(1, 4)]
    for partner in partners:
        pl.semaphore_signal(barrier, inc=1, device_id=partner, device_id_type=MESH)

    expert = lax.broadcasted_iota(jnp.int32, (EXPERTS, TOK), 0)
    first, second = ids_ref[0:1, :] == expert, ids_ref[1:2, :] == expert
    chosen = jnp.where(first | second, 1.0, 0.0)
    earlier = lax.broadcasted_iota(jnp.int32, (TOK, TOK), 0) < lax.broadcasted_iota(
        jnp.int32, (TOK, TOK), 1
    )
    position = jnp.dot(
        chosen.astype(BF16),
        jnp.where(earlier, 1.0, 0.0).astype(BF16),
        preferred_element_type=F32,
    )
    shift = (c * CAP).astype(F32)
    meta[0, c, 0:8, :] = jnp.where(first | second, position + shift, -1.0)
    meta[0, c, 8:16, :] = jnp.where(first, probs_ref[0:1, :], 0.0) + jnp.where(
        second, probs_ref[1:2, :], 0.0
    )

    pl.semaphore_wait(barrier, len(partners))

    mine = pl.ds(pl.multiple_of(c * TOK, TOK), TOK)
    theirs = pl.ds(pl.multiple_of(other * TOK, TOK), TOK)
    for copy in load_own:
        copy.wait()
    swap = remote(own.at[other], tokens.at[0, mine], other_core)
    swap.start()
    swap_in = remote(own.at[other], tokens.at[0, theirs], other_core, used[0] - 1)
    swap_meta = remote(meta.at[0, c], meta.at[0, c], other_core)
    swap_meta.start()
    swap_meta_in = remote(meta.at[0, other], meta.at[0, other], other_core, used[0] - 1)
    keep = local(own.at[c], tokens.at[0, mine])
    keep.start()
    swap_meta_in.wait_recv()
    swap_in.wait_recv()
    keep.wait()

    even = 1 - lax.rem(z, 2)
    near = lax.rem(z + 9 - 2 * even, 8)
    far = lax.rem(z + 4 * even + 6, 8)
    columns = [pl.ds(piece * WIDE, WIDE) for piece in range(PIECES)]

    def along_z(source, slot, target):
        return [remote(meta.at[source], meta.at[slot], at_z(target))] + [
            remote(tokens.at[source, :, part], tokens.at[slot, :, part], at_z(target))
            for part in columns
        ]

    z_near, z_far = along_z(0, 1, near), along_z(0, 2, far)
    z_next = along_z(1, 3, far)
    arrival = [None, z_near, z_far, z_next]
    for one, two in zip(z_near, z_far):
        one.start()
        two.start()

    half = zh // 2
    up, down = lax.rem(y + 1, 4), lax.rem(y + 3, 4)
    onward = lax.rem(y + 1 + 2 * c, 4)
    slot_of = lax.broadcasted_iota(jnp.int32, (BLOCK, TOK), 0).astype(F32)
    core_weight = c.astype(F32)

    def block_rows(chunk, step):
        return pl.ds(chunk * CHUNK + step * BLOCK, BLOCK)

    y_sent, y_passed, core_sent, core_got = {}, {}, {}, {}
    for chunk in range(4):
        for piece in range(PIECES):
            part, slot = columns[piece], chunk % 2
            y_sent[chunk, piece] = [
                remote(
                    ready.at[slot, 0, :, part],
                    rows.at[c, block_rows(chunk, 1), part],
                    at_y(up),
                ),
                remote(ready.at[slot, 1, :, part], passing.at[chunk, :, part], at_y(onward)),
                remote(
                    ready.at[slot, 2, :, part],
                    rows.at[c, block_rows(chunk, 3), part],
                    at_y(down),
                ),
            ]
            y_passed[chunk, piece] = remote(
                passing.at[chunk, :, part],
                rows.at[c, block_rows(chunk, 2), part],
                at_y(onward),
            )
            whole = pl.ds(chunk * CHUNK, CHUNK)
            core_sent[chunk, piece] = remote(
                rows.at[c, whole, part], rows.at[c, whole, part], other_core
            )
            core_got[chunk, piece] = remote(
                rows.at[other, whole, part], rows.at[other, whole, part], other_core, used[0] - 1
            )

    def send_rows(chunk, piece):
        part = columns[piece]
        for step in (2, 1, 3, 0):
            name = lax.rem(y + step, 4) * 2 + half
            hot = [
                meta[chunk, core, pl.ds(name, 1), :] == slot_of for core in range(2)
            ]
            hot = [jnp.where(one, 1.0, 0.0) for one in hot]
            weight = sum(
                jnp.sum(one * meta[chunk, core, pl.ds(name + 8, 1), :], axis=1, keepdims=True)
                for core, one in enumerate(hot)
            )
            scale = weight * core_weight + (1.0 - core_weight)
            picked = jnp.dot(
                jnp.concatenate(hot, axis=1).astype(BF16),
                tokens[chunk, :, part],
                preferred_element_type=F32,
            )
            picked = (picked * scale).astype(BF16)
            if step == 0:
                rows[c, block_rows(chunk, 0), part] = picked
            else:
                if chunk >= 2:
                    y_sent[chunk - 2, piece][step - 1].wait_send()
                ready[chunk % 2, step - 1, :, part] = picked
                y_sent[chunk, piece][step - 1].start()

    def pass_rows(chunk, piece):
        y_sent[chunk, piece][1].wait_recv()
        y_passed[chunk, piece].start()

    def share_rows(chunk, piece):
        y_sent[chunk, piece][0].wait_recv()
        y_sent[chunk, piece][2].wait_recv()
        y_passed[chunk, piece].wait_recv()
        core_sent[chunk, piece].start()

    for piece in range(PIECES):
        send_rows(0, piece)

    swap.wait_send()
    load_attn = local(attn_hbm, own.at[0])
    load_attn.start()
    load_latent.wait()
    load_attn.wait()

    @pl.loop(0, TOK // 16)
    def _(tile):
        part = pl.ds(pl.multiple_of(tile * 16, 16), 16)
        values = own[0, part, :].astype(F32)
        inv_rms = lax.rsqrt(jnp.mean(values * values, axis=1, keepdims=True) + epsilon)
        own[1, part, :] = (values * inv_rms * gain_ref[...]).astype(BF16)

    work[896:904, 0:KVL] = jnp.zeros((8, KVL), F32)

    @pl.loop(0, 4)
    def _(tile):
        normed = own[1, :, pl.ds(pl.multiple_of(tile * PAIR, 128), PAIR)]
        work[0:896, 0:KVL] = lax.dot_general(
            normed, latent[...], (((0,), (0,)), ((), ())), preferred_element_type=F32
        )
        start = lax.rem(tile, 2) * 4096 + (tile // 2) * 64
        for place in range(64):
            fixed = (place % 2) * 8192 + (place // 8) * 512 + (place % 8 // 2) * 128
            share = work[14 * place : 14 * place + 16, 0:KVL].astype(BF16)
            for lane in range(4):
                to = pl.multiple_of(start + fixed + lane * 16, 16)
                parts[pl.ds(to, 16), :] = share[:, lane * 128 : lane * 128 + 128]

    def half_of(core):
        return pl.multiple_of(core * 8192, 8192)

    kv_to_core = remote(parts.at[pl.ds(half_of(other), 8192)], kv_core, other_core)
    kv_to_core.start()

    for piece in range(PIECES):
        pass_rows(0, piece)

    kv_to_core.wait_recv()

    @pl.loop(0, 16)
    def _(tile):
        at = pl.multiple_of(tile * 512, 512)
        here = pl.ds(half_of(c) + at, 512)
        parts[here, :] = (
            parts[here, :].astype(F32) + kv_core[pl.ds(at, 512), :].astype(F32)
        ).astype(BF16)

    kv_to_x = []
    for step in range(1, 4):
        target = lax.rem(x + step, 4)
        at = pl.ds(half_of(c) + pl.multiple_of(target * 2048, 2048), 2048)
        kv_to_x.append(remote(parts.at[at], kv_x.at[step - 1], at_x(target)))
        kv_to_x[-1].start()

    for piece in range(PIECES):
        share_rows(0, piece)

    z_near[0].wait_recv()
    z_next[0].start()
    for piece in range(PIECES):
        z_near[1 + piece].wait_recv()
        z_next[1 + piece].start()
        send_rows(1, piece)

    for copy in kv_to_x:
        copy.wait()

    @pl.loop(0, 4)
    def _(tile):
        at = pl.multiple_of(tile * 512, 512)
        total = parts[pl.ds(half_of(c) + pl.multiple_of(x * 2048, 2048) + at, 512), :].astype(F32)
        for step in range(3):
            total = total + kv_x[step, pl.ds(at, 512), :].astype(F32)
        kv_x_sum[pl.ds(at, 512), :] = total.astype(BF16)

    kv_to_y = []
    for step in range(1, 4):
        target = lax.rem(y + step, 4)
        at = pl.ds(pl.multiple_of(target * 512, 512), 512)
        kv_to_y.append(remote(kv_x_sum.at[at], kv_y.at[step - 1], at_y(target)))
        kv_to_y[-1].start()

    for piece in range(PIECES):
        pass_rows(1, piece)
    for piece in range(PIECES):
        share_rows(1, piece)

    for copy in kv_to_y:
        copy.wait()
    total = kv_x_sum[pl.ds(pl.multiple_of(y * 512, 512), 512), :].astype(F32)
    for step in range(3):
        total = total + kv_y[step].astype(F32)
    kv_y_sum[...] = total.astype(BF16)
    kv_to_z = []
    for step in range(1, 8):
        target = lax.rem(z + step, 8)
        at = pl.ds(pl.multiple_of(target * 64, 64), 64)
        kv_to_z.append(remote(kv_y_sum.at[at], kv_z.at[step - 1], at_z(target)))
        kv_to_z[-1].start()

    z_far[0].wait_recv()
    for piece in range(PIECES):
        z_far[1 + piece].wait_recv()
        send_rows(2, piece)

    def hidden_units(part):
        for chunk in (2 * part, 2 * part + 1):
            for piece in range(PIECES):
                core_got[chunk, piece].wait_recv()
        group = pl.ds(part * 2 * CHUNK, 2 * CHUNK)
        tall = 2 * CHUNK
        work[0:tall, 0 : 3 * FQ] = jnp.zeros((tall, 3 * FQ), F32)

        @pl.loop(0, 7)
        def _(tile):
            at = pl.ds(pl.multiple_of(tile * 512, 512), 512)
            work[0:tall, 0 : 2 * FQ] += jnp.dot(
                rows[0, group, at], w_gate_up[at, :], preferred_element_type=F32
            )
            work[0:tall, 2 * FQ : 3 * FQ] += lax.dot_general(
                rows[1, group, at],
                w_down[:, at],
                (((1,), (1,)), ((), ())),
                preferred_element_type=F32,
            )

        @pl.loop(0, tall // 128)
        def _(tile):
            at = pl.ds(pl.multiple_of(tile * 128, 128), 128)
            to = pl.ds(pl.multiple_of(part * tall + tile * 128, 128), 128)
            gate, up_proj = work[at, 0:FQ], work[at, FQ : 2 * FQ]
            back = work[at, 2 * FQ : 3 * FQ]
            sigmoid = jax.nn.sigmoid(gate)
            active = gate * sigmoid * up_proj
            up_rows = back * gate * sigmoid
            gate_rows = back * up_proj * sigmoid * (1.0 + gate * (1.0 - sigmoid))
            hidden_t[0:FQ, to] = gate_rows.T.astype(BF16)
            hidden_t[FQ : 2 * FQ, to] = up_rows.T.astype(BF16)
            hidden_t[2 * FQ : 3 * FQ, to] = active.T.astype(BF16)

    for copy in load_later:
        copy.wait()
    hidden_units(0)

    for piece in range(PIECES):
        pass_rows(2, piece)
    for piece in range(PIECES):
        share_rows(2, piece)

    z_next[0].wait_recv()
    for piece in range(PIECES):
        z_next[1 + piece].wait_recv()
        send_rows(3, piece)

    for copy in kv_to_z:
        copy.wait()
    total = kv_y_sum[pl.ds(pl.multiple_of(z * 64, 64), 64), :].astype(F32)
    for step in range(7):
        total = total + kv_z[step].astype(F32)
    for lane in range(4):
        kv_out[:, lane * 128 : lane * 128 + 128] = total[lane * 16 : lane * 16 + 16, :]
    kv_to_core.wait_send()

    for piece in range(PIECES):
        pass_rows(3, piece)
    for piece in range(PIECES):
        share_rows(3, piece)
    hidden_units(1)

    right, left, across = lax.rem(x + 1, 4), lax.rem(x + 3, 4), lax.rem(x + 2, 4)

    def slice_at(which):
        return pl.ds(pl.multiple_of(which * SLICE, SLICE), SLICE)

    low = lax.broadcasted_iota(jnp.int32, (384, 128), 1) < 64

    def gradients(pair):
        at = pl.ds(pl.multiple_of(pair * PAIR, 128), PAIR)
        work[0 : 2 * FQ, :] = jnp.dot(
            hidden_t[0 : 2 * FQ, :], rows[0, :, at], preferred_element_type=F32
        )
        work[2 * FQ : 3 * FQ, :] = jnp.dot(
            hidden_t[2 * FQ : 3 * FQ, :], rows[1, :, at], preferred_element_type=F32
        )
        start = pair * 2 * SLICE

        def put(which, block, value):
            to = pl.multiple_of(start + which * SLICE + block * 384, 128)
            parts[pl.ds(to, 384), :] = value.astype(BF16)

        for lane in range(3):
            for tall in range(2):
                high = slice(tall * 384, tall * 384 + 384)
                put(0, tall * 3 + lane, work[high, lane * 128 : lane * 128 + 128])
                put(1, tall * 3 + lane, work[high, 512 + lane * 128 : 640 + lane * 128])
        top, bottom = work[0:384, 384:512], pltpu.roll(work[384:768, 384:512], 64, 1)
        put(0, 6, jnp.where(low, top, bottom))
        put(1, 6, jnp.where(low, bottom, top))

    side = x // 2
    gradients(1 - side)
    to_right = remote(parts.at[slice_at(across)], first_sums.at[0], at_x(right))
    to_right.start()
    gradients(3 - side)
    to_left = remote(parts.at[slice_at(4 + across)], first_sums.at[1], at_x(left))
    to_left.start()
    gradients(side)
    gradients(2 + side)
    plain_right = remote(parts.at[slice_at(4 + right)], second_sums.at[2], at_x(right))
    plain_left = remote(parts.at[slice_at(left)], second_sums.at[1], at_x(left))
    plain_right.start()
    plain_left.start()

    def add_into(which, *added):
        @pl.loop(0, 7)
        def _(tile):
            at = pl.multiple_of(tile * 384, 128)
            here = pl.ds(pl.multiple_of(which * SLICE, 128) + at, 384)
            total = parts[here, :].astype(F32)
            for one in added:
                total = total + one[pl.ds(at, 384), :].astype(F32)
            parts[here, :] = total.astype(BF16)

    to_right.wait_recv()
    add_into(right, first_sums.at[0])
    sum_right = remote(parts.at[slice_at(right)], second_sums.at[0], at_x(right))
    sum_right.start()
    to_left.wait_recv()
    add_into(4 + left, first_sums.at[1])
    sum_left = remote(parts.at[slice_at(4 + left)], second_sums.at[3], at_x(left))
    sum_left.start()

    for copy in (plain_right, plain_left, sum_right, sum_left):
        copy.wait_recv()
    far_half = 1 - zl
    add_into(far_half * 4 + x, second_sums.at[far_half * 2], second_sums.at[far_half * 2 + 1])
    to_zl = remote(parts.at[slice_at(far_half * 4 + x)], last_sum, other_zl)
    to_zl.start()
    to_zl.wait_recv()
    mine_at = pl.multiple_of((zl * 4 + x) * SLICE, 128)
    for block in range(7):
        at = pl.ds(block * 384, 384)
        total = parts[pl.ds(mine_at + block * 384, 384), :].astype(F32)
        total = total + second_sums[zl * 2, at, :].astype(F32)
        total = total + second_sums[zl * 2 + 1, at, :].astype(F32)
        work[0:384, block * 128 : block * 128 + 128] = total + last_sum[at, :].astype(F32)
    store = local(work.at[pl.ds(0, 384)], terms_out)
    store.start()

    for copy in (swap_meta, to_right, to_left, plain_right, plain_left, sum_right, sum_left, to_zl):
        copy.wait_send()
    for group in (z_near, z_far, z_next):
        for copy in group:
            copy.wait_send()
    for chunk in range(4):
        for piece in range(PIECES):
            if chunk >= 2:
                for copy in y_sent[chunk, piece]:
                    copy.wait_send()
            y_passed[chunk, piece].wait_send()
            core_sent[chunk, piece].wait_send()
    store.wait()


def run_kernel(ids, probs, gain, *arrays):
    vmem, any_space = pl.BlockSpec(memory_space=pltpu.VMEM), pl.BlockSpec(memory_space=pl.ANY)
    return pl.pallas_call(
        kernel,
        out_shape=(
            jax.ShapeDtypeStruct((16, KVL), F32),
            jax.ShapeDtypeStruct((384, PAIR), F32),
        ),
        in_specs=[vmem] * 3 + [any_space] * len(arrays),
        out_specs=(vmem, any_space),
        scratch_shapes=[
            pltpu.VMEM((2, TOK, D), BF16),
            pltpu.VMEM((4, 2 * TOK, D), BF16),
            pltpu.VMEM((4, 2, 16, TOK), F32),
            pltpu.VMEM((2, 3, BLOCK, D), BF16),
            pltpu.VMEM((4, BLOCK, D), BF16),
            pltpu.VMEM((2, ROWS, D), BF16),
            pltpu.VMEM((D, 2 * FQ), BF16),
            pltpu.VMEM((FQ, D), BF16),
            pltpu.VMEM((TOK, KVL), BF16),
            pltpu.VMEM((3 * FQ, ROWS), BF16),
            pltpu.VMEM((904, PAIR), F32),
            pltpu.VMEM((8 * SLICE, 128), BF16),
            pltpu.VMEM((2, SLICE, 128), BF16),
            pltpu.VMEM((4, SLICE, 128), BF16),
            pltpu.VMEM((SLICE, 128), BF16),
            pltpu.VMEM((8192, 128), BF16),
            pltpu.VMEM((3, 2048, 128), BF16),
            pltpu.VMEM((2048, 128), BF16),
            pltpu.VMEM((3, 512, 128), BF16),
            pltpu.VMEM((512, 128), BF16),
            pltpu.VMEM((7, 64, 128), BF16),
            pltpu.SemaphoreType.DMA((COPIES,)),
            pltpu.SemaphoreType.DMA((COPIES,)),
            pltpu.SemaphoreType.DMA((10,)),
        ],
        compiler_params=pltpu.CompilerParams(
            collective_id=0, has_side_effects=True, vmem_limit_bytes=63 << 20
        ),
        cost_estimate=pl.CostEstimate(
            flops=2 * ROWS * D * FQ * 6, bytes_accessed=12 << 20, transcendentals=ROWS * FQ
        ),
        name="expert_gradients",
    )(ids, probs, gain, *arrays)


def body(
    attn_input,
    kv_gain,
    latent_cot,
    attn_resid,
    moe_input,
    moe_cot,
    expert_ids,
    gate_probs,
    w_gate,
    w_up,
    w_down,
    gate_resid,
    up_resid,
    down_resid,
):
    latent_sum, terms = run_kernel(
        expert_ids.T,
        gate_probs.T,
        kv_gain[None, :],
        moe_input,
        moe_cot,
        attn_input,
        latent_cot,
        w_gate,
        w_up,
        w_down,
    )
    kv_grad = (latent_sum[:14] + attn_resid).astype(BF16)
    even = lax.rem(lax.axis_index("edp_1"), 2) == 0
    main = jnp.concatenate([terms[:, :384], terms[:, 384:768]], axis=0)
    lower, upper = terms[:, 768:832], terms[:, 832:896]
    edge = jnp.concatenate(
        [jnp.where(even, lower, upper), jnp.where(even, upper, lower)], axis=0
    )
    summed = jnp.where(
        even, jnp.concatenate([main, edge], axis=1), jnp.concatenate([edge, main], axis=1)
    )
    gate_grad = (summed[:FQ].T + gate_resid).astype(BF16)
    up_grad = (summed[FQ : 2 * FQ].T + up_resid).astype(BF16)
    down_grad = (summed[2 * FQ :] + down_resid).astype(BF16)
    return (kv_grad, gate_grad, up_grad, down_grad)


def solution(mesh):
    torus = Mesh(mesh.devices.reshape(2, 4, 4, 4, 2), ("edp_0", "edp_1", "ep_0", "ep_1", "ep_2"))
    return jax.shard_map(
        body,
        mesh=torus,
        in_specs=(
            P(EDP_EP, None),
            P(),
            P(EDP_EP, None),
            P(EDP_EP, None),
            P(EDP_EP, None),
            P(EDP_EP, None),
            P(EDP_EP, None),
            P(EDP_EP, None),
            P(None, EP),
            P(None, EP),
            P(EP, None),
            P(EDP, EP),
            P(EDP, EP),
            P(EP, EDP),
        ),
        out_specs=(P(EDP_EP, None), P(EDP, EP), P(EDP, EP), P(EP, EDP)),
        check_vma=False,
    )
```

time: 666 us -> 282 us (0.42)
  waiting for transfers between devices: 531 us -> 0 us
  Pallas kernels: 0 us -> 271 us
  matrix products: 52.5 us -> 0 us
  local copies, waits for them, and re-layouts: 36.2 us -> 7.27 us
  starting transfers between devices: 20 us -> 0 us
  between operations: 15.9 us -> 0.73 us
    all_to_all x2 -> x0, waiting for transfers between devices: 361 us -> none  [the longest x1 201 us: body(): lax.all_to_all(sent_in, EP, split_axis=0, concat_axis=0, tiled=True)]
    pallas_call x0 -> x1, Pallas kernels: none -> 271 us  [run_kernel(): pl.pallas_call(kernel, out_shape=(jax.ShapeDtypeStruct((16, KVL), F32), j...]
    unnamed x6 -> x0, waiting for transfers between devices: 147 us -> none
    dot_general x10 -> x0, matrix products: 52.5 us -> none  [the longest x4 28.2 us: contract_rows(): lax.dot_general(left, right, (((0,), (0,)), ((), ())), preferred_element_...]
    reduce_scatter x4 -> x0, waiting for transfers between devices: 22.9 us -> none  [the longest x1 22.9 us: summed_rows(): parts = lax.psum_scatter(parts, core, scatter_dimension=0, tiled=True)]
    all_to_all x2 -> x0, starting transfers between devices: 19.3 us -> none  [the longest x1 12.9 us: body(): lax.all_to_all(sent_in, EP, split_axis=0, concat_axis=0, tiled=True)]
    transpose x1 -> x0, local copies, waits for them, and re-layouts: 10.6 us -> none  [summed_rows(): parts = parts.reshape(*sizes, *inside).swapaxes(0, 1).reshape(-1, *inside)]
    another operation x1 -> x0, local copies, waits for them, and re-layouts: 8.99 us -> none  [summed_rows(): parts = parts.reshape(*sizes, *inside).swapaxes(0, 1).reshape(-1, *inside)]
  transfers between devices with their start and end apart: 7 -> 0, of which waited for: 4 -> 0; matrix products, arithmetic and copies ran while one was open for 12% -> 0% of each run, Pallas kernels for 0% -> 0%
where the time goes in v1:
time: 282 us; the launch traced here: 281 us
  Pallas kernels  271 us (96%)
  local copies, waits for them, and re-layouts  7.27 us (3%)
    pallas_call x1, Pallas kernels, run_kernel(): pl.pallas_call(kernel, out_shape=(jax.ShapeDtypeStruct((16, KVL), F32), j...  271 us

profile of v1, /device:TPU:1, one launch (start us, length us, event | category | flops | bytes accessed | tf_op | source)
XLA Modules:
  0.0 281.3 jit_solution(1628199098149007264)
XLA Ops:
  0.6 1.3 broadcast_in_dim.3.gain_ref
  2.0 270.7 %expert_gradients.1 = (f32[16,512]{1,0:T(8,128)}, f32[384,896]{1,0:T(8,128)}) custom-call(s32[2,128]{1,0:T(2,128)} %bitcast.14, f32[2,128]{1,0:T(2,128)} %bitcast.15, f32[1,3584]{1,0:T(1,128)} %broadcast_in_dim.3.gain_ref, bf16[128,3584]{1,0:T(8,128)(2,1)} %input_hbm.1, bf16[128,3584]{1,0:T(8,128)(2,1)} %cot_hbm.1, bf16[128,3584]{1,0:T(8,128)(2,1)} %attn_hbm.1, ...), custom_call_target="tpu_custom_call" | custom-call | flops 14092861440 | bytes 12582912 | tf_op jit(solution)/shard_map/expert_gradients/pallas_call | solution.py:523
  272.7 1.1 slice_select_fusion.1
  273.9 1.3 fusion.5
  275.2 0.0 copy-start
  275.2 0.0 copy-start.1
  275.2 0.5 maximum_select_fusion
  275.7 0.5 copy-done
  276.2 0.2 copy.18
  276.4 0.0 copy-done.1
  276.4 0.2 copy.19
  276.6 0.3 fusion.2
  276.9 0.8 copy.21
  277.7 0.0 copy-start.2
  277.7 0.0 copy-start.3
  277.7 0.8 copy.22
  278.6 1.2 copy.20
  279.8 0.1 fusion
  279.9 0.8 copy.23
  280.7 0.0 copy-done.2
  280.7 0.0 copy-done.3
  280.7 0.6 add_convert_fusion
Async XLA Ops:
  275.2 1.0 copy-start
  275.2 1.2 copy-start.1
  277.7 3.0 %copy-start.2 = (f32[14,512]{1,0:T(8,128)S(1)}, f32[14,512]{1,0:T(8,128)}, u32[]{:S(2)}) copy-start(f32[14,512]{1,0:T(8,128)} %param.17) | copy-start | bytes 86020
  277.7 3.0 %copy-start.3 = (f32[16,512]{1,0:T(8,128)S(1)}, f32[16,512]{1,0:T(8,128)}, u32[]{:S(2)}) copy-start(f32[16,512]{1,0:T(8,128)} %get-tuple-element.6) | copy-start | bytes 98308

commit v2 on v1

--- a/solution.py
+++ b/solution.py
@@ -19,11 +19,14 @@
 BLOCK = 2 * CAP
 CHUNK = 4 * BLOCK
 ROWS = 4 * CHUNK
-PIECES = 2
+PIECES = 4
 WIDE = D // PIECES
 PAIR = 896
 SLICE = 2688
-COPIES = 96
+EARLY = 1536
+LATE = SLICE - EARLY
+TURN = LATE // 2
+COPIES = 136
 
 
 def kernel(
@@ -38,7 +41,7 @@
     w_up_hbm,
     w_down_hbm,
     kv_out,
-    terms_out,
+    sums_out,
     own,
     tokens,
     meta,
@@ -51,9 +54,12 @@
     hidden_t,
     work,
     parts,
-    first_sums,
-    second_sums,
-    last_sum,
+    early_first,
+    early_sums,
+    early_zl,
+    late_zl,
+    late_first,
+    late_sums,
     kv_core,
     kv_x,
     kv_x_sum,
@@ -169,10 +175,8 @@
 
     z_near, z_far = along_z(0, 1, near), along_z(0, 2, far)
     z_next = along_z(1, 3, far)
-    arrival = [None, z_near, z_far, z_next]
-    for one, two in zip(z_near, z_far):
-        one.start()
-        two.start()
+    for copy in z_near:
+        copy.start()
 
     half = zh // 2
     up, down = lax.rem(y + 1, 4), lax.rem(y + 3, 4)
@@ -312,10 +316,14 @@
         share_rows(0, piece)
 
     z_near[0].wait_recv()
-    z_next[0].start()
     for piece in range(PIECES):
         z_near[1 + piece].wait_recv()
-        z_next[1 + piece].start()
+        if piece == PIECES - 2:
+            z_far[0].start()
+            z_far[1].start()
+        if piece == PIECES - 1:
+            for copy in z_far[2:]:
+                copy.start()
         send_rows(1, piece)
 
     for copy in kv_to_x:
@@ -357,14 +365,21 @@
     z_far[0].wait_recv()
     for piece in range(PIECES):
         z_far[1 + piece].wait_recv()
+        if piece == PIECES - 2:
+            for copy in z_next[:3]:
+                copy.start()
+        if piece == PIECES - 1:
+            for copy in z_next[3:]:
+                copy.start()
         send_rows(2, piece)
-
-    def hidden_units(part):
-        for chunk in (2 * part, 2 * part + 1):
+        if piece:
+            pass_rows(2, piece - 1)
+
+    def hidden_units(start, tall, chunks):
+        for chunk in chunks:
             for piece in range(PIECES):
                 core_got[chunk, piece].wait_recv()
-        group = pl.ds(part * 2 * CHUNK, 2 * CHUNK)
-        tall = 2 * CHUNK
+        group = pl.ds(start, tall)
         work[0:tall, 0 : 3 * FQ] = jnp.zeros((tall, 3 * FQ), F32)
 
         @pl.loop(0, 7)
@@ -383,7 +398,7 @@
         @pl.loop(0, tall // 128)
         def _(tile):
             at = pl.ds(pl.multiple_of(tile * 128, 128), 128)
-            to = pl.ds(pl.multiple_of(part * tall + tile * 128, 128), 128)
+            to = pl.ds(pl.multiple_of(start + tile * 128, 128), 128)
             gate, up_proj = work[at, 0:FQ], work[at, FQ : 2 * FQ]
             back = work[at, 2 * FQ : 3 * FQ]
             sigmoid = jax.nn.sigmoid(gate)
@@ -396,17 +411,11 @@
 
     for copy in load_later:
         copy.wait()
-    hidden_units(0)
-
-    for piece in range(PIECES):
-        pass_rows(2, piece)
+    hidden_units(0, 2 * CHUNK, (0, 1))
+
+    pass_rows(2, PIECES - 1)
     for piece in range(PIECES):
         share_rows(2, piece)
-
-    z_next[0].wait_recv()
-    for piece in range(PIECES):
-        z_next[1 + piece].wait_recv()
-        send_rows(3, piece)
 
     for copy in kv_to_z:
         copy.wait()
@@ -417,16 +426,30 @@
         kv_out[:, lane * 128 : lane * 128 + 128] = total[lane * 16 : lane * 16 + 16, :]
     kv_to_core.wait_send()
 
-    for piece in range(PIECES):
-        pass_rows(3, piece)
+    z_next[0].wait_recv()
+    for piece in range(PIECES):
+        z_next[1 + piece].wait_recv()
+        send_rows(3, piece)
+        if piece:
+            pass_rows(3, piece - 1)
+    pass_rows(3, PIECES - 1)
+    hidden_units(2 * CHUNK, 256, (2,))
     for piece in range(PIECES):
         share_rows(3, piece)
-    hidden_units(1)
-
-    right, left, across = lax.rem(x + 1, 4), lax.rem(x + 3, 4), lax.rem(x + 2, 4)
-
-    def slice_at(which):
-        return pl.ds(pl.multiple_of(which * SLICE, SLICE), SLICE)
+    hidden_units(2 * CHUNK + 256, 2 * CHUNK - 256, (3,))
+
+    across, far_half = lax.rem(x + 2, 4), 1 - zl
+    side = x // 2
+    turns = [lax.rem(x + 1, 4), lax.rem(x + 3, 4)]
+
+    def early(which):
+        return pl.ds(pl.multiple_of(which * SLICE, 128), EARLY)
+
+    def late(which, turn=None):
+        at = which * SLICE + EARLY
+        if turn is None:
+            return pl.ds(pl.multiple_of(at, 128), LATE)
+        return pl.ds(pl.multiple_of(at + turn * TURN, 64), TURN)
 
     low = lax.broadcasted_iota(jnp.int32, (384, 128), 1) < 64
 
@@ -453,57 +476,148 @@
         put(0, 6, jnp.where(low, top, bottom))
         put(1, 6, jnp.where(low, bottom, top))
 
-    side = x // 2
-    gradients(1 - side)
-    to_right = remote(parts.at[slice_at(across)], first_sums.at[0], at_x(right))
-    to_right.start()
-    gradients(3 - side)
-    to_left = remote(parts.at[slice_at(4 + across)], first_sums.at[1], at_x(left))
-    to_left.start()
-    gradients(side)
-    gradients(2 + side)
-    plain_right = remote(parts.at[slice_at(4 + right)], second_sums.at[2], at_x(right))
-    plain_left = remote(parts.at[slice_at(left)], second_sums.at[1], at_x(left))
-    plain_right.start()
-    plain_left.start()
-
-    def add_into(which, *added):
-        @pl.loop(0, 7)
+    def onward_x(half):
+        return lax.rem(x + 1 + 2 * half, 4)
+
+    def back_x(half):
+        return lax.rem(x + 3 + 2 * half, 4)
+
+    def add_rows(start, count, tile_rows, *added):
+        @pl.loop(0, count // tile_rows)
         def _(tile):
-            at = pl.multiple_of(tile * 384, 128)
-            here = pl.ds(pl.multiple_of(which * SLICE, 128) + at, 384)
+            at = pl.multiple_of(tile * tile_rows, 64)
+            here = pl.ds(pl.multiple_of(start + at, 64), tile_rows)
             total = parts[here, :].astype(F32)
             for one in added:
-                total = total + one[pl.ds(at, 384), :].astype(F32)
+                total = total + one[pl.ds(at, tile_rows), :].astype(F32)
             parts[here, :] = total.astype(BF16)
 
-    to_right.wait_recv()
-    add_into(right, first_sums.at[0])
-    sum_right = remote(parts.at[slice_at(right)], second_sums.at[0], at_x(right))
-    sum_right.start()
-    to_left.wait_recv()
-    add_into(4 + left, first_sums.at[1])
-    sum_left = remote(parts.at[slice_at(4 + left)], second_sums.at[3], at_x(left))
-    sum_left.start()
-
-    for copy in (plain_right, plain_left, sum_right, sum_left):
+    sums_sent = []
+
+    def send(src, dst, device):
+        copy = remote(src, dst, device)
+        copy.start()
+        sums_sent.append(copy)
+        return copy
+
+    def send_zl(target):
+        return send(parts.at[late(far_half * 4 + target)], late_zl.at[target], other_zl)
+
+    def send_across(half):
+        return send(
+            parts.at[early(half * 4 + across)], early_first.at[half], at_x(onward_x(half))
+        )
+
+    zl_sent = {}
+    gradients(far_half * 2 + 1 - side)
+    for place in range(2):
+        zl_sent[place] = send_zl((1 - side) * 2 + place)
+    far_across = send_across(far_half)
+    gradients(zl * 2 + 1 - side)
+    near_across = send_across(zl)
+    gradients(far_half * 2 + side)
+    for place in range(2):
+        zl_sent[2 + place] = send_zl(side * 2 + place)
+    gradients(zl * 2 + side)
+    plain = [
+        send(
+            parts.at[early(half * 4 + back_x(half))],
+            early_sums.at[half, 1],
+            at_x(back_x(half)),
+        )
+        for half in (far_half, zl)
+    ]
+    merged = []
+    for half, copy in ((far_half, far_across), (zl, near_across)):
         copy.wait_recv()
-    far_half = 1 - zl
-    add_into(far_half * 4 + x, second_sums.at[far_half * 2], second_sums.at[far_half * 2 + 1])
-    to_zl = remote(parts.at[slice_at(far_half * 4 + x)], last_sum, other_zl)
-    to_zl.start()
-    to_zl.wait_recv()
-    mine_at = pl.multiple_of((zl * 4 + x) * SLICE, 128)
-    for block in range(7):
+        ahead = half * 4 + onward_x(half)
+        add_rows(ahead * SLICE, EARLY, 384, early_first.at[half])
+        merged.append(
+            send(parts.at[early(ahead)], early_sums.at[half, 0], at_x(onward_x(half)))
+        )
+
+    for copy in zl_sent.values():
+        copy.wait_recv()
+
+    def take_zl(target):
+        add_rows((zl * 4 + target) * SLICE + EARLY, LATE, 384, late_zl.at[target])
+
+    def turn_rows(turn):
+        return pl.ds(turn * TURN, TURN)
+
+    take_zl(across)
+    late_across = [
+        send(
+            parts.at[late(zl * 4 + across, turn)], late_first.at[turn_rows(turn)], at_x(turns[turn])
+        )
+        for turn in range(2)
+    ]
+    for target in turns:
+        take_zl(target)
+    late_plain = [
+        send(
+            parts.at[late(zl * 4 + turns[1 - turn], turn)],
+            late_sums.at[1, turn_rows(turn)],
+            at_x(turns[1 - turn]),
+        )
+        for turn in range(2)
+    ]
+    take_zl(x)
+
+    for copy in (plain[0], merged[0]):
+        copy.wait_recv()
+    here = far_half * 4 + x
+    add_rows(
+        here * SLICE, EARLY, 384, early_sums.at[far_half, 0], early_sums.at[far_half, 1]
+    )
+    early_last = send(parts.at[early(here)], early_zl, other_zl)
+
+    late_merged = []
+    for turn in range(2):
+        late_across[turn].wait_recv()
+        ahead = zl * 4 + turns[turn]
+        add_rows(
+            ahead * SLICE + EARLY + turn * TURN, TURN, 192, late_first.at[turn_rows(turn)]
+        )
+        late_merged.append(
+            send(
+                parts.at[late(ahead, turn)], late_sums.at[0, turn_rows(turn)], at_x(turns[turn])
+            )
+        )
+
+    mine_at = (zl * 4 + x) * SLICE
+
+    def put_sum(block, added):
+        total = parts[pl.ds(pl.multiple_of(mine_at + block * 384, 128), 384), :].astype(F32)
+        for one in added:
+            total = total + one.astype(F32)
+        work[0:384, block * 128 : block * 128 + 128] = total
+
+    for copy in (plain[1], merged[1], early_last):
+        copy.wait_recv()
+    for block in range(4):
         at = pl.ds(block * 384, 384)
-        total = parts[pl.ds(mine_at + block * 384, 384), :].astype(F32)
-        total = total + second_sums[zl * 2, at, :].astype(F32)
-        total = total + second_sums[zl * 2 + 1, at, :].astype(F32)
-        work[0:384, block * 128 : block * 128 + 128] = total + last_sum[at, :].astype(F32)
-    store = local(work.at[pl.ds(0, 384)], terms_out)
+        put_sum(block, (early_sums[zl, 0, at, :], early_sums[zl, 1, at, :], early_zl[at, :]))
+    for copy in late_plain + late_merged:
+        copy.wait_recv()
+    for block in range(3):
+        at = pl.ds(block * 384, 384)
+        put_sum(4 + block, (late_sums[0, at, :], late_sums[1, at, :]))
+
+    odd = lax.rem(x, 2)
+    main = pl.ds(pl.multiple_of(384 + odd * 64, 64), 384)
+    edge = pl.ds(pl.multiple_of(768 - odd * 384, 64), 64)
+    edges = work[0:384, 768:896].T
+    swapped = lax.broadcasted_iota(jnp.int32, (64, 384), 0) * 0 + odd == 1
+    work[edge, 0:384] = jnp.where(swapped, edges[64:128, :], edges[0:64, :])
+    work[edge, 384:768] = jnp.where(swapped, edges[0:64, :], edges[64:128, :])
+    for tall in range(2):
+        high = slice(tall * 384, tall * 384 + 384)
+        work[main, high] = work[0:384, high].T
+    store = local(work.at[pl.ds(384, 448), pl.ds(0, 768)], sums_out)
     store.start()
 
-    for copy in (swap_meta, to_right, to_left, plain_right, plain_left, sum_right, sum_left, to_zl):
+    for copy in [swap_meta] + sums_sent:
         copy.wait_send()
     for group in (z_near, z_far, z_next):
         for copy in group:
@@ -524,7 +638,7 @@
         kernel,
         out_shape=(
             jax.ShapeDtypeStruct((16, KVL), F32),
-            jax.ShapeDtypeStruct((384, PAIR), F32),
+            jax.ShapeDtypeStruct((448, 3 * FQ), F32),
         ),
         in_specs=[vmem] * 3 + [any_space] * len(arrays),
         out_specs=(vmem, any_space),
@@ -541,9 +655,12 @@
             pltpu.VMEM((3 * FQ, ROWS), BF16),
             pltpu.VMEM((904, PAIR), F32),
             pltpu.VMEM((8 * SLICE, 128), BF16),
-            pltpu.VMEM((2, SLICE, 128), BF16),
-            pltpu.VMEM((4, SLICE, 128), BF16),
-            pltpu.VMEM((SLICE, 128), BF16),
+            pltpu.VMEM((2, EARLY, 128), BF16),
+            pltpu.VMEM((2, 2, EARLY, 128), BF16),
+            pltpu.VMEM((EARLY, 128), BF16),
+            pltpu.VMEM((4, LATE, 128), BF16),
+            pltpu.VMEM((LATE, 128), BF16),
+            pltpu.VMEM((2, LATE, 128), BF16),
             pltpu.VMEM((8192, 128), BF16),
             pltpu.VMEM((3, 2048, 128), BF16),
             pltpu.VMEM((2048, 128), BF16),
@@ -552,7 +669,7 @@
             pltpu.VMEM((7, 64, 128), BF16),
             pltpu.SemaphoreType.DMA((COPIES,)),
             pltpu.SemaphoreType.DMA((COPIES,)),
-            pltpu.SemaphoreType.DMA((10,)),
+            pltpu.SemaphoreType.DMA((12,)),
         ],
         compiler_params=pltpu.CompilerParams(
             collective_id=0, has_side_effects=True, vmem_limit_bytes=63 << 20
@@ -580,7 +697,7 @@
     up_resid,
     down_resid,
 ):
-    latent_sum, terms = run_kernel(
+    latent_sum, sums = run_kernel(
         expert_ids.T,
         gate_probs.T,
         kv_gain[None, :],
@@ -593,18 +710,9 @@
         w_down,
     )
     kv_grad = (latent_sum[:14] + attn_resid).astype(BF16)
-    even = lax.rem(lax.axis_index("edp_1"), 2) == 0
-    main = jnp.concatenate([terms[:, :384], terms[:, 384:768]], axis=0)
-    lower, upper = terms[:, 768:832], terms[:, 832:896]
-    edge = jnp.concatenate(
-        [jnp.where(even, lower, upper), jnp.where(even, upper, lower)], axis=0
-    )
-    summed = jnp.where(
-        even, jnp.concatenate([main, edge], axis=1), jnp.concatenate([edge, main], axis=1)
-    )
-    gate_grad = (summed[:FQ].T + gate_resid).astype(BF16)
-    up_grad = (summed[FQ : 2 * FQ].T + up_resid).astype(BF16)
-    down_grad = (summed[2 * FQ :] + down_resid).astype(BF16)
+    gate_grad = (sums[:, :FQ] + gate_resid).astype(BF16)
+    up_grad = (sums[:, FQ : 2 * FQ] + up_resid).astype(BF16)
+    down_grad = (sums[:, 2 * FQ :] + down_resid.T).astype(BF16).T
     return (kv_grad, gate_grad, up_grad, down_grad)
 
 

time: 282 us -> 207 us (0.73)
  Pallas kernels: 271 us -> 201 us
  local copies, waits for them, and re-layouts: 7.27 us -> 1.34 us
    pallas_call x1, Pallas kernels: 271 us -> 201 us  [run_kernel(): pl.pallas_call(kernel, out_shape=(jax.ShapeDtypeStruct((16, KVL), F32), j...]
    unnamed x14 -> x6, local copies, waits for them, and re-layouts: 4.62 us -> 0.01 us
where the time goes in v2:
time: 207 us
  Pallas kernels  201 us (97%)
  other arithmetic  3.71 us (2%)
    pallas_call x1, Pallas kernels, run_kernel(): pl.pallas_call(kernel, out_shape=(jax.ShapeDtypeStruct((16, KVL), F32), j...  201 us

profile of v2, /device:TPU:1, one launch (start us, length us, event | category | flops | bytes accessed | tf_op | source)
XLA Modules:
  0.0 206.8 jit_solution(9375596384598616517)
XLA Ops:
  0.6 1.3 broadcast_in_dim.3.gain_ref
  2.0 0.0 copy-start.2
  2.0 0.0 copy-start
  2.0 0.0 copy-start.1
  2.0 201.1 %expert_gradients.1 = (f32[16,512]{1,0:T(8,128)}, f32[448,768]{1,0:T(8,128)}) custom-call(s32[2,128]{1,0:T(2,128)} %bitcast.10, f32[2,128]{1,0:T(2,128)} %bitcast.11, f32[1,3584]{1,0:T(1,128)} %broadcast_in_dim.3.gain_ref, bf16[128,3584]{1,0:T(8,128)(2,1)} %input_hbm.1, bf16[128,3584]{1,0:T(8,128)(2,1)} %cot_hbm.1, bf16[128,3584]{1,0:T(8,128)(2,1)} %attn_hbm.1, ...), custom_call_target="tpu_custom_call" | custom-call | flops 14092861440 | bytes 12582912 | tf_op jit(solution)/shard_map/expert_gradients/pallas_call | solution.py:637
  203.1 0.0 copy-done.2
  203.1 1.4 add_convert_fusion.2
  204.5 0.0 copy-done
  204.5 0.0 copy-done.1
  204.5 2.3 %fusion.1 = (bf16[256,448]{0,1:T(8,128)(2,1)}, bf16[448,256]{1,0:T(8,128)(2,1)}, bf16[448,256]{1,0:T(8,128)(2,1)}) fusion(f32[256,448]{0,1:T(8,128)S(1)} %copy-done, f32[448,768]{1,0:T(8,128)} %get-tuple-element.7, f32[448,256]{1,0:T(8,128)S(1)} %copy-done.1, f32[448,256]{1,0:T(8,128)} %param.25), kind=kLoop, calls=%fused_computation.4 | loop fusion | flops 688128 | bytes 3440640 | tf_op jit(solution)/shard_map/transpose | solution.py:715
Async XLA Ops:
  2.0 201.1 %copy-start.2 = (f32[14,512]{1,0:T(8,128)S(1)}, f32[14,512]{1,0:T(8,128)}, u32[]{:S(2)}) copy-start(f32[14,512]{1,0:T(8,128)} %param.17) | copy-start | bytes 86020
  2.0 202.5 %copy-start = (f32[256,448]{0,1:T(8,128)S(1)}, f32[256,448]{0,1:T(8,128)}, u32[]{:S(2)}) copy-start(f32[256,448]{0,1:T(8,128)} %param.27) | copy-start | bytes 1376260
  2.0 202.5 %copy-start.1 = (f32[448,256]{1,0:T(8,128)S(1)}, f32[448,256]{1,0:T(8,128)}, u32[]{:S(2)}) copy-start(f32[448,256]{1,0:T(8,128)} %param.26) | copy-start | bytes 1376260

commit v3 on v2

--- a/solution.py
+++ b/solution.py
@@ -20,19 +20,20 @@
 CHUNK = 4 * BLOCK
 ROWS = 4 * CHUNK
 PIECES = 4
-WIDE = D // PIECES
+BOUNDS = (0, 896, 1792, 2688, D)
+TILE = 896
 PAIR = 896
 SLICE = 2688
 EARLY = 1536
 LATE = SLICE - EARLY
 TURN = LATE // 2
-COPIES = 136
+COPIES = 144
 
 
 def kernel(
     ids_ref,
     probs_ref,
-    gain_ref,
+    gain_hbm,
     input_hbm,
     cot_hbm,
     attn_hbm,
@@ -51,6 +52,7 @@
     w_gate_up,
     w_down,
     latent,
+    gain,
     hidden_t,
     work,
     parts,
@@ -115,8 +117,8 @@
         local(w_up_hbm, w_gate_up.at[:, pl.ds(FQ, FQ)]),
         local(w_down_hbm, w_down),
     ]
-    load_latent = local(latent_hbm, latent)
-    for copy in load_own + load_later + [load_latent]:
+    load_latent = [local(latent_hbm, latent), local(gain_hbm, gain.at[0])]
+    for copy in load_own + load_later + load_latent:
         copy.start()
 
     barrier = pltpu.get_barrier_semaphore()
@@ -148,33 +150,33 @@
 
     mine = pl.ds(pl.multiple_of(c * TOK, TOK), TOK)
     theirs = pl.ds(pl.multiple_of(other * TOK, TOK), TOK)
+    columns = [pl.ds(at, to - at) for at, to in zip(BOUNDS, BOUNDS[1:])]
+
+    even = 1 - lax.rem(z, 2)
+    near = lax.rem(z + 9 - 2 * even, 8)
+    far = lax.rem(z + 4 * even + 6, 8)
+
     for copy in load_own:
         copy.wait()
+    swap_meta = remote(meta.at[0, c], meta.at[0, c], other_core)
+    swap_meta.start()
+    swap_meta_in = remote(meta.at[0, other], meta.at[0, other], other_core, used[0] - 1)
     swap = remote(own.at[other], tokens.at[0, mine], other_core)
     swap.start()
     swap_in = remote(own.at[other], tokens.at[0, theirs], other_core, used[0] - 1)
-    swap_meta = remote(meta.at[0, c], meta.at[0, c], other_core)
-    swap_meta.start()
-    swap_meta_in = remote(meta.at[0, other], meta.at[0, other], other_core, used[0] - 1)
     keep = local(own.at[c], tokens.at[0, mine])
     keep.start()
     swap_meta_in.wait_recv()
     swap_in.wait_recv()
     keep.wait()
 
-    even = 1 - lax.rem(z, 2)
-    near = lax.rem(z + 9 - 2 * even, 8)
-    far = lax.rem(z + 4 * even + 6, 8)
-    columns = [pl.ds(piece * WIDE, WIDE) for piece in range(PIECES)]
-
     def along_z(source, slot, target):
         return [remote(meta.at[source], meta.at[slot], at_z(target))] + [
             remote(tokens.at[source, :, part], tokens.at[slot, :, part], at_z(target))
             for part in columns
         ]
 
-    z_near, z_far = along_z(0, 1, near), along_z(0, 2, far)
-    z_next = along_z(1, 3, far)
+    z_near, z_far, z_next = along_z(0, 1, near), along_z(0, 2, far), along_z(1, 3, far)
     for copy in z_near:
         copy.start()
 
@@ -260,7 +262,8 @@
     swap.wait_send()
     load_attn = local(attn_hbm, own.at[0])
     load_attn.start()
-    load_latent.wait()
+    for copy in load_latent:
+        copy.wait()
     load_attn.wait()
 
     @pl.loop(0, TOK // 16)
@@ -268,7 +271,7 @@
         part = pl.ds(pl.multiple_of(tile * 16, 16), 16)
         values = own[0, part, :].astype(F32)
         inv_rms = lax.rsqrt(jnp.mean(values * values, axis=1, keepdims=True) + epsilon)
-        own[1, part, :] = (values * inv_rms * gain_ref[...]).astype(BF16)
+        own[1, part, :] = (values * inv_rms * gain[...]).astype(BF16)
 
     work[896:904, 0:KVL] = jnp.zeros((8, KVL), F32)
 
@@ -375,16 +378,16 @@
         if piece:
             pass_rows(2, piece - 1)
 
-    def hidden_units(start, tall, chunks):
+    def hidden_piece(start, tall, chunks, piece):
         for chunk in chunks:
-            for piece in range(PIECES):
-                core_got[chunk, piece].wait_recv()
+            core_got[chunk, piece].wait_recv()
         group = pl.ds(start, tall)
-        work[0:tall, 0 : 3 * FQ] = jnp.zeros((tall, 3 * FQ), F32)
-
-        @pl.loop(0, 7)
+        if piece == 0:
+            work[0:tall, 0 : 3 * FQ] = jnp.zeros((tall, 3 * FQ), F32)
+
+        @pl.loop(BOUNDS[piece] // TILE, BOUNDS[piece + 1] // TILE)
         def _(tile):
-            at = pl.ds(pl.multiple_of(tile * 512, 512), 512)
+            at = pl.ds(pl.multiple_of(tile * TILE, TILE), TILE)
             work[0:tall, 0 : 2 * FQ] += jnp.dot(
                 rows[0, group, at], w_gate_up[at, :], preferred_element_type=F32
             )
@@ -395,6 +398,7 @@
                 preferred_element_type=F32,
             )
 
+    def hidden_end(start, tall):
         @pl.loop(0, tall // 128)
         def _(tile):
             at = pl.ds(pl.multiple_of(tile * 128, 128), 128)
@@ -409,6 +413,11 @@
             hidden_t[FQ : 2 * FQ, to] = up_rows.T.astype(BF16)
             hidden_t[2 * FQ : 3 * FQ, to] = active.T.astype(BF16)
 
+    def hidden_units(start, tall, chunks):
+        for piece in range(PIECES):
+            hidden_piece(start, tall, chunks, piece)
+        hidden_end(start, tall)
+
     for copy in load_later:
         copy.wait()
     hidden_units(0, 2 * CHUNK, (0, 1))
@@ -427,16 +436,18 @@
     kv_to_core.wait_send()
 
     z_next[0].wait_recv()
+    last = (2 * CHUNK + 256, 2 * CHUNK - 256)
     for piece in range(PIECES):
         z_next[1 + piece].wait_recv()
         send_rows(3, piece)
-        if piece:
-            pass_rows(3, piece - 1)
-    pass_rows(3, PIECES - 1)
-    hidden_units(2 * CHUNK, 256, (2,))
-    for piece in range(PIECES):
+        if piece >= 1:
+            hidden_piece(*last, (3,), piece - 1)
+        pass_rows(3, piece)
+        if piece == 0:
+            hidden_units(2 * CHUNK, 256, (2,))
         share_rows(3, piece)
-    hidden_units(2 * CHUNK + 256, 2 * CHUNK - 256, (3,))
+    hidden_piece(*last, (3,), PIECES - 1)
+    hidden_end(*last)
 
     across, far_half = lax.rem(x + 2, 4), 1 - zl
     side = x // 2
@@ -619,9 +630,8 @@
 
     for copy in [swap_meta] + sums_sent:
         copy.wait_send()
-    for group in (z_near, z_far, z_next):
-        for copy in group:
-            copy.wait_send()
+    for copy in z_near + z_far + z_next:
+        copy.wait_send()
     for chunk in range(4):
         for piece in range(PIECES):
             if chunk >= 2:
@@ -640,7 +650,7 @@
             jax.ShapeDtypeStruct((16, KVL), F32),
             jax.ShapeDtypeStruct((448, 3 * FQ), F32),
         ),
-        in_specs=[vmem] * 3 + [any_space] * len(arrays),
+        in_specs=[vmem] * 2 + [any_space] * (1 + len(arrays)),
         out_specs=(vmem, any_space),
         scratch_shapes=[
             pltpu.VMEM((2, TOK, D), BF16),
@@ -652,6 +662,7 @@
             pltpu.VMEM((D, 2 * FQ), BF16),
             pltpu.VMEM((FQ, D), BF16),
             pltpu.VMEM((TOK, KVL), BF16),
+            pltpu.VMEM((1, D), F32),
             pltpu.VMEM((3 * FQ, ROWS), BF16),
             pltpu.VMEM((904, PAIR), F32),
             pltpu.VMEM((8 * SLICE, 128), BF16),
@@ -669,7 +680,7 @@
             pltpu.VMEM((7, 64, 128), BF16),
             pltpu.SemaphoreType.DMA((COPIES,)),
             pltpu.SemaphoreType.DMA((COPIES,)),
-            pltpu.SemaphoreType.DMA((12,)),
+            pltpu.SemaphoreType.DMA((16,)),
         ],
         compiler_params=pltpu.CompilerParams(
             collective_id=0, has_side_effects=True, vmem_limit_bytes=63 << 20
@@ -700,7 +711,7 @@
     latent_sum, sums = run_kernel(
         expert_ids.T,
         gate_probs.T,
-        kv_gain[None, :],
+        kv_gain,
         moe_input,
         moe_cot,
         attn_input,

time: 207 us -> 203 us (0.981)
  Pallas kernels: 201 us -> 198 us
    pallas_call x1, Pallas kernels: 201 us -> 198 us  [run_kernel(): pl.pallas_call(kernel, out_shape=(jax.ShapeDtypeStruct((16, KVL), F32), j...]
where the time goes in v3:
time: 203 us
  Pallas kernels  198 us (98%)
  other arithmetic  3.71 us (2%)
    pallas_call x1, Pallas kernels, run_kernel(): pl.pallas_call(kernel, out_shape=(jax.ShapeDtypeStruct((16, KVL), F32), j...  198 us

profile of v3, /device:TPU:1, one launch (start us, length us, event | category | flops | bytes accessed | tf_op | source)
XLA Modules:
  0.0 202.8 jit_solution(16303813599525254434)
XLA Ops:
  0.6 0.0 copy-start.2
  0.6 0.0 copy-start
  0.7 0.0 copy-start.1
  0.7 198.4 %expert_gradients.1 = (f32[16,512]{1,0:T(8,128)}, f32[448,768]{1,0:T(8,128)}) custom-call(s32[2,128]{1,0:T(2,128)} %bitcast.10, f32[2,128]{1,0:T(2,128)} %bitcast.11, f32[3584]{0:T(1024)} %gain_hbm.1, bf16[128,3584]{1,0:T(8,128)(2,1)} %input_hbm.1, bf16[128,3584]{1,0:T(8,128)(2,1)} %cot_hbm.1, bf16[128,3584]{1,0:T(8,128)(2,1)} %attn_hbm.1, ...), custom_call_target="tpu_custom_call" | custom-call | flops 14092861440 | bytes 12582912 | tf_op jit(solution)/shard_map/expert_gradients/pallas_call | solution.py:647
  199.0 0.0 copy-done.2
  199.1 1.4 add_convert_fusion.2
  200.4 0.0 copy-done
  200.4 0.0 copy-done.1
  200.4 2.3 %fusion.1 = (bf16[256,448]{0,1:T(8,128)(2,1)}, bf16[448,256]{1,0:T(8,128)(2,1)}, bf16[448,256]{1,0:T(8,128)(2,1)}) fusion(f32[256,448]{0,1:T(8,128)S(1)} %copy-done, f32[448,768]{1,0:T(8,128)} %get-tuple-element.7, f32[448,256]{1,0:T(8,128)S(1)} %copy-done.1, f32[448,256]{1,0:T(8,128)} %param.25), kind=kLoop, calls=%fused_computation.4 | loop fusion | flops 688128 | bytes 3440640 | tf_op jit(solution)/shard_map/transpose | solution.py:726
Async XLA Ops:
  0.6 198.4 %copy-start.2 = (f32[14,512]{1,0:T(8,128)S(1)}, f32[14,512]{1,0:T(8,128)}, u32[]{:S(2)}) copy-start(f32[14,512]{1,0:T(8,128)} %param.17) | copy-start | bytes 86020
  0.6 199.8 %copy-start = (f32[256,448]{0,1:T(8,128)S(1)}, f32[256,448]{0,1:T(8,128)}, u32[]{:S(2)}) copy-start(f32[256,448]{0,1:T(8,128)} %param.27) | copy-start | bytes 1376260
  0.7 199.8 %copy-start.1 = (f32[448,256]{1,0:T(8,128)S(1)}, f32[448,256]{1,0:T(8,128)}, u32[]{:S(2)}) copy-start(f32[448,256]{1,0:T(8,128)} %param.26) | copy-start | bytes 1376260
